TPU v7x, 32 devices: a whole 2x2x4 slice. The times are simulated.
32 devices in a mesh: band: 8 (over z, x), coef: 4 (over y, core).
Axes of the slice: x: 2, y: 2, z: 4, core: 2. Of those that a mesh axis runs over, the one named last changes fastest.
Arguments:
- coeffs: float32 [1024, 262144], P('band', 'coef'), may hold values from -320 to 320
- ref_block: float32 [1024, 262144], P('band', 'coef'), may hold values from -0.01171875 to 0.01171875
- index_map: int32 [262144], P('coef'), may hold values from 0 to 65535, as said below
- band_group: int32 [1024], P('band'), may hold values from 0 to 15
Outputs:
- ortho: float32 [1024, 262144], P('band', 'coef')
- band_residual: float32 [1024], P('band')
- group_residual: float32 [16], replicated
Inputs may be any that keep to these rules, and one draw needn't show every extreme that they name: Within each aligned slab of 65536 coefficients, index_map holds every number of 0 to 65535 once.
All inputs are finite; a program needn't handle non-finite values.
Results may differ from a plain program's by a relative error of at most 0.000098.
Values sent between devices are 32-bit elements; how exact they have to be, the bound alone decides.
A program may use at most 384 MiB of HBM per device.

v0:
```python
import jax
import jax.numpy as jnp
from jax import lax
from jax.sharding import PartitionSpec as P

NB = 1024
NGROUPS = 16


def local(coeffs, ref_block, index_map, band_group):
    columns = lax.all_to_all(coeffs, "band", split_axis=1, concat_axis=0, tiled=True)
    partial_value = jnp.dot(
        columns, columns.T, precision=lax.Precision.HIGHEST, preferred_element_type=jnp.float32
    )
    margin = lax.psum(partial_value, ("band", "coef"))
    factor = jnp.linalg.cholesky(margin)
    ortho_cols = lax.linalg.triangular_solve(factor, columns, left_side=True, lower=True)
    ortho = lax.all_to_all(ortho_cols, "band", split_axis=0, concat_axis=1, tiled=True)
    aligned = jnp.take(ortho, index_map, axis=1)
    squares = jnp.sum((aligned - ref_block) ** 2, axis=1)
    group_range = jnp.arange(NGROUPS, dtype=jnp.int32)
    totals = lax.psum(squares, "coef")
    band_residual = jnp.sqrt(totals + 1e-06)
    onehot = (band_group[:, None] == group_range[None, :]).astype(jnp.float32)
    terms = jnp.dot(
        band_residual, onehot, precision=lax.Precision.HIGHEST, preferred_element_type=jnp.float32
    )
    group_residual = lax.psum(terms, "band") * (NGROUPS / NB)
    return (ortho, band_residual, group_residual)


def solution(mesh):
    return jax.shard_map(
        local,
        mesh=mesh,
        in_specs=(P("band", "coef"), P("band", "coef"), P("coef"), P("band")),
        out_specs=(P("band", "coef"), P("band"), P()),
        check_vma=False,
    )
```

profile of v0, /device:TPU:0, one launch (start us, length us, event | category | flops | bytes accessed | tf_op | source)
XLA Modules:
  0.0 2639.6 jit_solution(11342121475017291769)
XLA Ops:
  7.2 33.4 %copy.17 = f32[128,65536]{0,1:T(8,128)} copy(f32[128,65536]{1,0:T(8,128)} %param.4) | data formatting | bytes 67108864 | tf_op args[0]
  40.6 31.1 %copy.18 = f32[128,8,8192]{2,0,1:T(8,128)} copy(f32[128,8,8192]{0,2,1:T(8,128)} %bitcast.156) | data formatting | bytes 67108864 | tf_op jit(solution)/shard_map/all_to_all | solution.py:11
  71.7 735.1 %all_to_all.38 = f32[128,8,8192]{2,0,1:T(8,128)} all-to-all(f32[128,8,8192]{2,0,1:T(8,128)} %copy.18), channel_id=1, replica_groups=mesh['band'=8,'coef'=4] {'band'}, dimensions={1} | all-to-all | bytes 67108864 | tf_op jit(solution)/shard_map/all_to_all | solution.py:11
  806.8 117.0 %fusion.74 = f32[1024,1024]{0,1:T(8,128)} fusion(f32[1024,8192]{1,0:T(8,128)} %bitcast.157), kind=kOutput, calls=%fused_computation.177 | convolution fusion | flops 103079215104 | bytes 37748736 | tf_op jit(solution)/shard_map/dot_general | solution.py:12
  923.9 141.9 %all-reduce.3.cloned.1.call-done = f32[1024,1024]{0,1:T(8,128)} async-done(((f32[1024,1024]{0,1:T(8,128)}), f32[1024,1024]{0,1:T(8,128)}) %all-reduce.3.cloned.1.call-update) | async-done | bytes 4194320 | tf_op jit(solution)/shard_map/psum | solution.py:15
  1065.7 5.5 copy.20
  1077.7 11.7 cholesky.223
  1089.5 9.8 custom-call.62
  1105.7 11.9 cholesky.244
  1118.2 9.8 custom-call.63
  1131.4 11.7 cholesky.468
  1144.4 9.8 custom-call.64
  1157.7 12.1 cholesky.487
  1171.0 9.8 custom-call.65
  1184.3 11.7 cholesky.506
  1197.3 10.0 custom-call.66
  1210.6 11.7 cholesky.526
  1223.6 9.8 custom-call.67
  1236.4 11.9 cholesky.546
  1249.6 9.8 custom-call.68
  1262.1 11.7 cholesky.564
  1280.8 4.8 select_select_fusion
  1285.6 23.2 while.1
  1308.8 79.0 %custom-call.69 = f32[8,128,128]{1,2,0:T(8,128)S(1)} custom-call(f32[8,128,128]{2,1,0:T(8,128)S(1)} %get-tuple-element.10), custom_call_target="InvertDiagBlocksLowerTriangular" | custom-call | tf_op jit(solution)/shard_map/triangular_solve | solution.py:17
  1387.8 12.6 constant_dynamic-update-slice_fusion.17
  1400.4 6.9 convolution_subtract_fusion.1
  1407.3 8.2 constant_dynamic-update-slice_fusion.16
  1415.5 7.7 convolution_subtract_fusion
  1423.2 8.4 constant_dynamic-update-slice_fusion.15
  1431.6 12.2 fusion.16
  1443.8 13.9 constant_dynamic-update-slice_fusion.14
  1457.7 14.1 fusion.19
  1471.8 12.5 constant_dynamic-update-slice_fusion.13
  1484.3 17.1 convolution_subtract_fusion.2
  1501.4 6.7 constant_dynamic-update-slice_fusion.12
  1508.2 19.3 convolution_subtract_fusion.4
  1527.5 5.8 constant_dynamic-update-slice_fusion.11
  1533.3 23.5 convolution_subtract_fusion.3
  1556.8 7.9 convolution_dynamic-update-slice_fusion
  1564.7 7.1 all-to-all-start.1
  1571.8 33.4 %copy.22 = f32[128,65536]{0,1:T(8,128)} copy(f32[128,65536]{1,0:T(8,128)} %param.5) | data formatting | bytes 67108864 | tf_op args[1]
  1605.4 687.3 %all-to-all-done.1 = f32[8,128,8192]{2,1,0:T(8,128)} async-done(((f32[8,128,8192]{2,1,0:T(8,128)}), f32[8,128,8192]{2,1,0:T(8,128)}, u32[]{:S(2)}, u32[]{:S(2)}) %all-to-all-start.1) | async-done | bytes 33554464 | tf_op jit(solution)/shard_map/all_to_all | solution.py:18
  2292.7 31.0 %copy.21 = f32[128,8,8192]{0,2,1:T(8,128)} copy(f32[128,8,8192]{2,0,1:T(8,128)} %bitcast.35) | data formatting | bytes 67108864 | tf_op jit(solution)/shard_map/all_to_all | solution.py:18
  2323.7 228.0 %gather_fusion = f32[65536,128]{1,0:T(8,128)} fusion(f32[128,65536]{0,1:T(8,128)} %bitcast.154, s32[65536]{0:T(1024)S(1)} %fusion.45), kind=kCustom, calls=%fused_computation | custom fusion | bytes 67371008 | tf_op jit(solution)/shard_map/jit(_take)/gather | solution.py:19
  2551.7 20.7 fusion.1
  2572.4 5.7 psum.22
  2578.3 33.5 %copy.23 = f32[128,65536]{1,0:T(8,128)} copy(f32[128,65536]{0,1:T(8,128)} %bitcast.155) | data formatting | bytes 67108864
  2611.7 20.3 psum.23
  (86 shorter events, 65.2 us)
Async XLA Ops:
  7.2 1058.6 %all-reduce.3.cloned.1.call-start = ((), (), s32[]{:S(2)}) async-start(), calls=%async_computation.2 | async-start | bytes 8388608 | tf_op jit(solution)/shard_map/psum | solution.py:15
  1075.7 2.0 copy-start.3
  1400.4 31.3 %copy-start = (f32[128,8192]{1,0:T(8,128)}, f32[128,8192]{1,0:T(8,128)S(1)}, u32[]{:S(2)}) copy-start(f32[128,8192]{1,0:T(8,128)S(1)} %get-tuple-element.79) | copy-start | bytes 12582916
  1415.5 16.1 copy-start.1
  1431.6 12.2 copy-start.2
  1564.7 728.0 %all-to-all-start.1 = ((f32[8,128,8192]{2,1,0:T(8,128)}), f32[8,128,8192]{2,1,0:T(8,128)}, u32[]{:S(2)}, u32[]{:S(2)}) async-start(f32[8,128,8192]{2,1,0:T(8,128)} %bitcast.166), calls=%async_computation.1 | async-start | bytes 67108864 | tf_op jit(solution)/shard_map/all_to_all | solution.py:18
  1571.8 33.4 %copy-start.4 = (s32[65536]{0:T(1024)S(1)}, s32[65536]{0:T(1024)}, u32[]{:S(2)}) copy-start(s32[65536]{0:T(1024)} %param.6) | copy-start | bytes 786436
  2551.7 26.4 copy-start.5
  2578.1 33.7 %copy-start.6 = (f32[128]{0:T(128)}, f32[128]{0:T(128)S(1)}, u32[]{:S(2)}) copy-start(f32[128]{0:T(128)S(1)} %add_sqrt_fusion) | copy-start | bytes 1540
Sparse Core Ops, SparseCore 0:
  924.0 141.7 all-reduce.2
where the time goes:
time: 2650 us; the launch traced here: 2640 us
  waiting for transfers between devices  829 us (31%)
  blocking collectives  761 us (29%)
  local copies, waits for them, and re-layouts  424 us (16%)
  matrix products  317 us (12%)
  other arithmetic  282 us (11%)
    all_to_all x1, blocking collectives, local(): lax.all_to_all(coeffs, 'band', split_axis=1, concat_axis=0, tiled=True)  735 us
    all_to_all x1, waiting for transfers between devices, local(): lax.all_to_all(ortho_cols, 'band', split_axis=0, concat_axis=1, tiled=True)  687 us
    gather x1, local copies, waits for them, and re-layouts, local(): aligned = jnp.take(ortho, index_map, axis=1)  228 us
    another operation x15, matrix products, local(): lax.linalg.triangular_solve(factor, columns, left_side=True, lower=True)  177 us
    another operation x30, other arithmetic, local(): factor = jnp.linalg.cholesky(margin)  172 us
    psum x1, waiting for transfers between devices, local(): margin = lax.psum(partial_value, ('band', 'coef'))  142 us
    dot_general x1, matrix products, local(): jnp.dot(columns, columns.T, precision=lax.Precision.HIGHEST, preferred_el...  117 us
    unnamed x17, local copies, waits for them, and re-layouts  102 us
  transfers between devices with their start and end apart: 2, of which 2 were waited for; matrix products, arithmetic and copies ran while one was open for 1% of the time, Pallas kernels for 0%

commit v1 on v0

--- a/solution.py
+++ b/solution.py
@@ -12,7 +12,9 @@
     partial_value = jnp.dot(
         columns, columns.T, precision=lax.Precision.HIGHEST, preferred_element_type=jnp.float32
     )
-    margin = lax.psum(partial_value, ("band", "coef"))
+    margin = partial_value
+    for axis in ("coef", "band"):
+        margin = lax.psum(margin, axis)
     factor = jnp.linalg.cholesky(margin)
     ortho_cols = lax.linalg.triangular_solve(factor, columns, left_side=True, lower=True)
     ortho = lax.all_to_all(ortho_cols, "band", split_axis=0, concat_axis=1, tiled=True)

time: 2650 us -> 2750 us (1.038)
  waiting for transfers between devices: 829 us -> 934 us
    psum x1 -> x2, waiting for transfers between devices: 142 us -> 245 us  [local(): margin = lax.psum(margin, axis)]
  transfers between devices with their start and end apart: 2 -> 3, of which waited for: 2 -> 3; matrix products, arithmetic and copies ran while one was open for 1% -> 1% of each run, Pallas kernels for 0% -> 0%
where the time goes in v1:
time: 2750 us; the launch traced here: 2740 us
  waiting for transfers between devices  934 us (34%)
  blocking collectives  761 us (28%)
  local copies, waits for them, and re-layouts  424 us (15%)
  matrix products  317 us (12%)
  other arithmetic  282 us (10%)
    all_to_all x1, blocking collectives, local(): lax.all_to_all(coeffs, 'band', split_axis=1, concat_axis=0, tiled=True)  735 us
    all_to_all x1, waiting for transfers between devices, local(): lax.all_to_all(ortho_cols, 'band', split_axis=0, concat_axis=1, tiled=True)  689 us
    psum x2, waiting for transfers between devices, local(): margin = lax.psum(margin, axis)  245 us
    gather x1, local copies, waits for them, and re-layouts, local(): aligned = jnp.take(ortho, index_map, axis=1)  228 us
    another operation x15, matrix products, local(): lax.linalg.triangular_solve(factor, columns, left_side=True, lower=True)  177 us
    another operation x30, other arithmetic, local(): factor = jnp.linalg.cholesky(margin)  172 us
    dot_general x1, matrix products, local(): jnp.dot(columns, columns.T, precision=lax.Precision.HIGHEST, preferred_el...  117 us
    unnamed x17, local copies, waits for them, and re-layouts  102 us
  transfers between devices with their start and end apart: 3, of which 3 were waited for; matrix products, arithmetic and copies ran while one was open for 1% of the time, Pallas kernels for 0%

profile of v1, /device:TPU:0, one launch (start us, length us, event | category | flops | bytes accessed | tf_op | source)
XLA Modules:
  0.0 2744.6 jit_solution(11511541795989000729)
XLA Ops:
  7.2 33.4 %copy.17 = f32[128,65536]{0,1:T(8,128)} copy(f32[128,65536]{1,0:T(8,128)} %param.4) | data formatting | bytes 67108864 | tf_op args[0]
  40.6 31.1 %copy.18 = f32[128,8,8192]{2,0,1:T(8,128)} copy(f32[128,8,8192]{0,2,1:T(8,128)} %bitcast.156) | data formatting | bytes 67108864 | tf_op jit(solution)/shard_map/all_to_all | solution.py:11
  71.7 735.1 %all_to_all.38 = f32[128,8,8192]{2,0,1:T(8,128)} all-to-all(f32[128,8,8192]{2,0,1:T(8,128)} %copy.18), channel_id=1, replica_groups=mesh['band'=8,'coef'=4] {'band'}, dimensions={1} | all-to-all | bytes 67108864 | tf_op jit(solution)/shard_map/all_to_all | solution.py:11
  806.8 117.0 %fusion.74 = f32[1024,1024]{0,1:T(8,128)} fusion(f32[1024,8192]{1,0:T(8,128)} %bitcast.157), kind=kOutput, calls=%fused_computation.177 | convolution fusion | flops 103079215104 | bytes 37748736 | tf_op jit(solution)/shard_map/dot_general | solution.py:12
  923.9 84.7 %all-reduce.4.cloned.1.call-done = f32[1024,1024]{0,1:T(8,128)} async-done(((f32[1024,1024]{0,1:T(8,128)}), f32[1024,1024]{0,1:T(8,128)}) %all-reduce.4.cloned.1.call-update) | async-done | bytes 4194320 | tf_op jit(solution)/shard_map/psum | solution.py:17
  1008.7 160.2 %all-reduce.6.cloned.1.call-done = f32[1024,1024]{0,1:T(8,128)} async-done(((f32[1024,1024]{0,1:T(8,128)}), f32[1024,1024]{0,1:T(8,128)}) %all-reduce.6.cloned.1.call-update) | async-done | bytes 4194320 | tf_op jit(solution)/shard_map/psum | solution.py:17
  1168.9 5.5 copy.20
  1180.9 11.7 cholesky.223
  1192.6 9.8 custom-call.62
  1208.8 11.9 cholesky.244
  1221.4 9.8 custom-call.63
  1234.5 11.7 cholesky.468
  1247.5 9.8 custom-call.64
  1260.8 12.1 cholesky.487
  1274.2 9.8 custom-call.65
  1287.4 11.7 cholesky.506
  1300.4 10.0 custom-call.66
  1313.8 11.7 cholesky.526
  1326.8 9.8 custom-call.67
  1339.6 11.9 cholesky.546
  1352.8 9.8 custom-call.68
  1365.2 11.7 cholesky.564
  1388.7 23.2 while.1
  1411.9 79.0 %custom-call.69 = f32[8,128,128]{1,2,0:T(8,128)S(1)} custom-call(f32[8,128,128]{2,1,0:T(8,128)S(1)} %get-tuple-element.10), custom_call_target="InvertDiagBlocksLowerTriangular" | custom-call | tf_op jit(solution)/shard_map/triangular_solve | solution.py:19
  1490.9 12.6 constant_dynamic-update-slice_fusion.17
  1503.5 6.9 convolution_subtract_fusion.1
  1510.4 8.2 constant_dynamic-update-slice_fusion.16
  1518.6 7.7 convolution_subtract_fusion
  1526.4 8.4 constant_dynamic-update-slice_fusion.15
  1534.8 12.2 fusion.16
  1547.0 13.9 constant_dynamic-update-slice_fusion.14
  1560.8 14.1 fusion.19
  1574.9 12.5 constant_dynamic-update-slice_fusion.13
  1587.4 17.1 convolution_subtract_fusion.2
  1604.6 6.7 constant_dynamic-update-slice_fusion.12
  1611.3 19.3 convolution_subtract_fusion.4
  1630.6 5.8 constant_dynamic-update-slice_fusion.11
  1636.4 23.5 convolution_subtract_fusion.3
  1659.9 7.9 convolution_dynamic-update-slice_fusion
  1667.9 7.1 all-to-all-start.1
  1674.9 33.4 %copy.22 = f32[128,65536]{0,1:T(8,128)} copy(f32[128,65536]{1,0:T(8,128)} %param.5) | data formatting | bytes 67108864 | tf_op args[1]
  1708.5 688.9 %all-to-all-done.1 = f32[8,128,8192]{2,1,0:T(8,128)} async-done(((f32[8,128,8192]{2,1,0:T(8,128)}), f32[8,128,8192]{2,1,0:T(8,128)}, u32[]{:S(2)}, u32[]{:S(2)}) %all-to-all-start.1) | async-done | bytes 33554464 | tf_op jit(solution)/shard_map/all_to_all | solution.py:20
  2397.4 31.0 %copy.21 = f32[128,8,8192]{0,2,1:T(8,128)} copy(f32[128,8,8192]{2,0,1:T(8,128)} %bitcast.35) | data formatting | bytes 67108864 | tf_op jit(solution)/shard_map/all_to_all | solution.py:20
  2428.4 228.0 %gather_fusion = f32[65536,128]{1,0:T(8,128)} fusion(f32[128,65536]{0,1:T(8,128)} %bitcast.154, s32[65536]{0:T(1024)S(1)} %fusion.45), kind=kCustom, calls=%fused_computation | custom fusion | bytes 67371008 | tf_op jit(solution)/shard_map/jit(_take)/gather | solution.py:21
  2656.4 20.7 fusion.1
  2677.1 5.7 psum.30
  2682.9 33.5 %copy.23 = f32[128,65536]{1,0:T(8,128)} copy(f32[128,65536]{0,1:T(8,128)} %bitcast.155) | data formatting | bytes 67108864
  2716.4 20.6 psum.31
  (89 shorter events, 70.0 us)
Async XLA Ops:
  7.2 1001.5 %all-reduce.4.cloned.1.call-start = ((), (), s32[]{:S(2)}) async-start(), calls=%async_computation.2 | async-start | bytes 8388608 | tf_op jit(solution)/shard_map/psum | solution.py:17
  923.8 245.0 %all-reduce.6.cloned.1.call-start = ((), (), s32[]{:S(2)}) async-start(), calls=%async_computation.3 | async-start | bytes 8388608 | tf_op jit(solution)/shard_map/psum | solution.py:17
  1178.8 2.0 copy-start.3
  1503.5 31.3 %copy-start = (f32[128,8192]{1,0:T(8,128)}, f32[128,8192]{1,0:T(8,128)S(1)}, u32[]{:S(2)}) copy-start(f32[128,8192]{1,0:T(8,128)S(1)} %get-tuple-element.79) | copy-start | bytes 12582916
  1518.6 16.1 copy-start.1
  1534.7 12.2 copy-start.2
  1667.9 729.5 %all-to-all-start.1 = ((f32[8,128,8192]{2,1,0:T(8,128)}), f32[8,128,8192]{2,1,0:T(8,128)}, u32[]{:S(2)}, u32[]{:S(2)}) async-start(f32[8,128,8192]{2,1,0:T(8,128)} %bitcast.166), calls=%async_computation.1 | async-start | bytes 67108864 | tf_op jit(solution)/shard_map/all_to_all | solution.py:20
  1674.9 33.4 %copy-start.4 = (s32[65536]{0:T(1024)S(1)}, s32[65536]{0:T(1024)}, u32[]{:S(2)}) copy-start(s32[65536]{0:T(1024)} %param.6) | copy-start | bytes 786436
  2656.4 26.4 copy-start.5
  2682.7 33.7 %copy-start.6 = (f32[128]{0:T(128)}, f32[128]{0:T(128)S(1)}, u32[]{:S(2)}) copy-start(f32[128]{0:T(128)S(1)} %add_sqrt_fusion) | copy-start | bytes 1540
Sparse Core Ops, SparseCore 0:
  924.0 84.6 all-reduce.3
  1012.3 156.5 all-reduce.5
